TPU v7x, 256 devices: a whole 4x4x8 slice. The times are simulated.
256 devices in a mesh: seq: 32 (over x, y, core), exp: 8 (over z).
Axes of the slice: x: 4, y: 4, z: 8, core: 2. Of those that a mesh axis runs over, the one named last changes fastest.
Arguments:
- tokens: bfloat16 [96, 4, 1024], P('exp'), may hold values from -48 to 48
- attn_gain: float32 [1024], replicated, may hold values from 0.1 to 1.9
- w_qkv: bfloat16 [3072, 1024], P('seq'), may hold values from -0.1875 to 0.1875
- window_cache: bfloat16 [2, 96, 4096, 1024], P(None, 'exp', 'seq'), may hold values from -180 to 180
- sink_cache: bfloat16 [2, 96, 4, 1024], P(None, 'exp'), may hold values from -6 to 6
- lengths: int32 [96], P('exp'), may hold values from 8 to 16384, as said below
- w_out: bfloat16 [1024, 1024], P('seq'), may hold values from -0.1875 to 0.1875
- moe_gain: float32 [1024], replicated, may hold values from 0.1 to 1.9
- router: bfloat16 [1024, 16], replicated, may hold values from -0.1875 to 0.1875
- expert_ids: int32 [96, 4, 2], P('exp'), may hold values from 0 to 15, all different within a row
- slot_order: int32 [8, 48], P('exp'), may hold values from 0 to 47, each once within a row
- expert_in: bfloat16 [2, 8, 5632, 1024], P(None, 'exp', 'seq'), may hold values from -0.1875 to 0.1875
- expert_down: bfloat16 [8, 5632, 1024], P('exp', 'seq'), may hold values from -0.109375 to 0.109375
Outputs:
- output: bfloat16 [96, 4, 1024], P('exp')
Inputs may be any that keep to these rules, and one draw needn't show every extreme that they name: `lengths`: at least one request holds 16384 tokens. `expert_ids`: the 2 experts of a token differ, and every expert is named by some token. `slot_order`: each group's row holds every number of 0 to 47 once.
All inputs are finite; a program needn't handle non-finite values.
Results may differ from a plain program's by a relative error of at most 0.0083.
The roundings to bfloat16 on the way count: a program that leaves them out, or rounds other values in their place, can miss the bound.
Values may be sent and summed in bfloat16 or wider, within the bound.
A program may use at most 64 MiB of HBM per device.

v0:
```python
import jax
import jax.numpy as jnp
from jax import lax
from jax.sharding import PartitionSpec as P

HEADS = 16
HD = 64
EXPERTS = 16
TOPK = 2
SINKS = 4
WIN = 4096
CAP = 8
EPSILON = 1e-06
MASKED = -1e30


def rms_scale(values, gain_row):
    widened = values.astype(jnp.float32)
    inverse = lax.rsqrt(jnp.mean(widened * widened, axis=-1, keepdims=True) + EPSILON)
    return (widened * inverse * gain_row).astype(jnp.bfloat16)


def by_heads(values, factor):
    shaped = values.reshape(factor.shape + (values.shape[-1] // factor.shape[-1],))
    return (shaped * factor[..., None]).reshape(values.shape)


def expert_tail(gate_up, down_rows, own_expert, local_experts):
    hidden = (jax.nn.gelu(gate_up[0], approximate=True) * gate_up[1]).astype(jnp.bfloat16)
    outputs = jnp.einsum("nkf,fd->nkd", hidden, down_rows, preferred_element_type=jnp.float32)
    placing = (jnp.arange(local_experts, dtype=jnp.int32) == own_expert).astype(jnp.float32)
    return outputs[:, None, :, :] * placing[None, :, None, None]


def body(
    tokens,
    attn_gain,
    w_qkv,
    window_cache,
    sink_cache,
    lengths,
    w_out,
    moe_gain,
    router,
    expert_ids,
    slot_order,
    expert_in,
    expert_down,
):
    requests, step_count, model_width = tokens.shape
    row_count = requests * step_count
    seq_index = lax.axis_index("seq")
    seq_count = lax.axis_size("seq")
    group_count = lax.axis_size("exp")
    local_experts = EXPERTS // group_count
    own_expert = seq_index // (seq_count // local_experts)
    in_rows = expert_in[:, 0]
    down_rows = expert_down[0]
    contract = (((1,), (1,)), ((), ()))
    flat_rows = tokens.reshape(row_count, model_width)
    normed_attn = rms_scale(flat_rows, attn_gain)
    local_mix = lax.dot_general(
        normed_attn, w_qkv, contract, preferred_element_type=jnp.float32
    ).astype(jnp.bfloat16)
    mixed_rows = lax.all_gather(local_mix, "seq", axis=1, tiled=True).reshape(
        requests, step_count, 3, HEADS, HD
    )
    queries = mixed_rows[:, :, 0]
    new_keys = mixed_rows[:, :, 1]
    new_values = mixed_rows[:, :, 2]
    score_scale = HD ** (-0.5)
    slot_span = window_cache.shape[2]
    slot_ids = seq_index * slot_span + jnp.arange(slot_span, dtype=jnp.int32)
    cache_keys = window_cache[0].reshape(requests, slot_span, HEADS, HD)
    cache_values = window_cache[1].reshape(requests, slot_span, HEADS, HD)
    window_scores = (
        jnp.einsum("rshe,rwhe->rshw", queries, cache_keys, preferred_element_type=jnp.float32)
        * score_scale
    )
    filled = jnp.minimum(WIN, lengths - SINKS)
    step_ids = jnp.arange(step_count, dtype=jnp.int32)
    written = (lengths[:, None] + step_ids[None, :] - SINKS) % WIN
    overwritten = (
        jnp.cumsum((slot_ids[None, None, :] == written[:, :, None]).astype(jnp.int32), axis=1) > 0
    )
    window_live = (
        (slot_ids[None, None, :] < filled[:, None, None]) & jnp.logical_not(overwritten)
    )[:, :, None, :]
    sink_keys = sink_cache[0].reshape(requests, SINKS, HEADS, HD)
    sink_values = sink_cache[1].reshape(requests, SINKS, HEADS, HD)
    local_keys = jnp.concatenate([sink_keys, new_keys], axis=1)
    local_values = jnp.concatenate([sink_values, new_values], axis=1)
    local_scores = (
        jnp.einsum("rshe,rkhe->rshk", queries, local_keys, preferred_element_type=jnp.float32)
        * score_scale
    )
    causal = jnp.concatenate(
        [jnp.ones((step_count, SINKS), jnp.bool_), step_ids[None, :] <= step_ids[:, None]], axis=1
    )
    local_live = causal[None, :, None, :] & (seq_index == 0)
    peak_score = jnp.maximum(
        jnp.max(jnp.where(window_live, window_scores, MASKED), axis=-1),
        jnp.max(jnp.where(local_live, local_scores, MASKED), axis=-1),
    )
    window_exp = jnp.where(window_live, jnp.exp(window_scores - peak_score[..., None]), 0.0)
    local_exp = jnp.where(local_live, jnp.exp(local_scores - peak_score[..., None]), 0.0)
    weight_sum = jnp.sum(window_exp, axis=-1) + jnp.sum(local_exp, axis=-1)
    weighted = jnp.einsum(
        "rshw,rwhe->rshe",
        window_exp.astype(jnp.bfloat16),
        cache_values,
        preferred_element_type=jnp.float32,
    )
    weighted = weighted + jnp.einsum(
        "rshk,rkhe->rshe",
        local_exp.astype(jnp.bfloat16),
        local_values,
        preferred_element_type=jnp.float32,
    )
    weighted = weighted.reshape(requests, step_count, model_width)
    overall = lax.pmax(peak_score, "seq")
    factor = jnp.exp(peak_score - overall)
    weight_sum, weighted = (
        lax.psum((weight_sum * factor).astype(jnp.bfloat16), "seq").astype(jnp.float32),
        lax.psum(by_heads(weighted, factor).astype(jnp.bfloat16), "seq").astype(jnp.float32),
    )
    attended = by_heads(weighted, 1.0 / weight_sum).astype(jnp.bfloat16)
    local_proj = lax.dot_general(
        attended.reshape(row_count, model_width),
        w_out,
        contract,
        preferred_element_type=jnp.float32,
    ).astype(jnp.bfloat16)
    projected = lax.all_gather(local_proj, "seq", axis=1, tiled=True)
    residual = flat_rows.astype(jnp.float32) + projected.astype(jnp.float32)
    normed_moe = rms_scale(residual, moe_gain)
    logits = jnp.dot(normed_moe, router, preferred_element_type=jnp.float32)
    chosen = expert_ids.reshape(row_count, TOPK)
    onehot = (chosen[:, :, None] == jnp.arange(EXPERTS, dtype=jnp.int32)).astype(jnp.float32)
    gate_values = jax.nn.sigmoid(jnp.sum(onehot * logits[:, None, :], axis=-1))
    priority = slot_order[0]
    earlier = (priority[None, :] < priority[:, None]).astype(jnp.float32)
    counts = jnp.dot(earlier, jnp.sum(onehot, axis=1), precision=lax.Precision.HIGHEST)
    position = jnp.sum(onehot * counts[:, None, :], axis=-1).astype(jnp.int32)
    column = chosen * CAP + position
    select = (
        (column[:, :, None] == jnp.arange(EXPERTS * CAP, dtype=jnp.int32))
        & (position < CAP)[:, :, None]
    ).astype(jnp.bfloat16)
    dispatch = jnp.sum(select, axis=1)
    buffer = lax.dot_general(
        dispatch, normed_moe, (((0,), (0,)), ((), ())), preferred_element_type=jnp.float32
    ).astype(jnp.bfloat16)
    buffer = buffer.reshape(group_count, local_experts, CAP, model_width)
    own_rows = lax.dynamic_index_in_dim(
        lax.all_to_all(buffer, "exp", split_axis=0, concat_axis=0, tiled=True),
        own_expert,
        1,
        keepdims=False,
    )
    gate_up = jnp.einsum("nkd,pfd->pnkf", own_rows, in_rows, preferred_element_type=jnp.float32)
    expert_part = expert_tail(gate_up, down_rows, own_expert, local_experts)
    summed = lax.psum(expert_part.astype(jnp.bfloat16), "seq")
    returned = lax.all_to_all(summed, "exp", split_axis=0, concat_axis=0, tiled=True).reshape(
        EXPERTS * CAP, model_width
    )
    picked = jnp.einsum("rkc,cd->rkd", select, returned, preferred_element_type=jnp.float32)
    final_rows = (residual + jnp.sum(gate_values[:, :, None] * picked, axis=1)).astype(jnp.bfloat16)
    result = final_rows.reshape(requests, step_count, model_width)
    return result


def solution(mesh):
    in_specs = (
        P("exp", None, None),
        P(),
        P("seq", None),
        P(None, "exp", "seq", None),
        P(None, "exp", None, None),
        P("exp"),
        P("seq", None),
        P(),
        P(),
        P("exp", None, None),
        P("exp", None),
        P(None, "exp", "seq", None),
        P("exp", "seq", None),
    )
    out_specs = P("exp", None, None)
    return jax.shard_map(body, mesh=mesh, in_specs=in_specs, out_specs=out_specs, check_vma=False)
```

profile of v0, /device:TPU:2, one launch (start us, length us, event | category | flops | bytes accessed | tf_op | source)
XLA Modules:
  0.0 496.3 jit_solution(1817082701008093470)
XLA Ops:
  6.5 0.8 add_select_fusion
  7.3 0.7 add_minimum_fusion
  8.0 0.9 reshape.165
  8.9 1.0 multiply_reduce_fusion.1
  10.2 6.6 %fusion.66 = (bf16[1,12,128,1024]{3,2,1,0:T(8,128)(2,1)}, bf16[1,12,128,1024]{3,2,1,0:T(8,128)(2,1)}) fusion(bf16[2,12,128,1024]{3,2,1,0:T(8,128)(2,1)} %param.16), kind=kLoop, calls=%fused_computation.111 | loop fusion | bytes 12582912 | tf_op jit(solution)/shard_map/slice | solution.py:75
  16.8 4.8 copy.86
  21.9 24.9 %all-gather = bf16[32,96,48]{1,2,0:T(8,128)(2,1)S(1)} all-gather(bf16[1,96,48]{1,2,0:T(8,128)(2,1)S(1)} %fusion.6), channel_id=1, replica_groups=mesh['seq'=32,'exp'=8] {'seq'}, dimensions={0}, use_global_device_ids=true | all-gather | bytes 304128 | tf_op jit(solution)/shard_map/all_gather | solution.py:65
  46.9 0.5 reshape.167
  47.4 0.4 reshape.160
  48.0 2.9 select_reduce_fusion.1
  51.6 0.5 select_reduce_fusion
  52.4 109.0 %pmax.7 = f32[12,4,16]{2,1,0:T(4,128)S(1)} all-reduce(f32[12,4,16]{2,1,0:T(4,128)S(1)} %max.9), channel_id=1, replica_groups=mesh['seq'=32,'exp'=8] {'seq'}, use_global_device_ids=true, to_apply=%region_4.5 | all-reduce | flops 768 | bytes 6144 | tf_op jit(solution)/shard_map/pmax | solution.py:121
  161.4 0.5 fusion.16
  162.0 0.5 fusion.18
  163.1 4.7 copy.92
  168.0 0.5 convolution_bitcast_fusion
  168.5 3.7 fusion.4
  172.3 0.8 convert_element_type.106
  173.1 123.8 %psum.22 = bf16[12,4,16]{2,1,0:T(4,128)(2,1)S(1)} all-reduce(bf16[12,4,16]{2,1,0:T(4,128)(2,1)S(1)} %get-tuple-element.7), channel_id=1, replica_groups=mesh['seq'=32,'exp'=8] {'seq'}, use_global_device_ids=true, to_apply=%region_8.9 | all-reduce | flops 768 | bytes 3072 | tf_op jit(solution)/shard_map/psum | solution.py:124
  297.8 0.6 all-reduce.4.cloned.1.call-done
  298.4 0.9 multiply_convert_fusion.2
  299.5 39.6 %all_gather.7 = bf16[48,1024]{0,1:T(8,128)(2,1)S(1)} all-gather(bf16[48,32]{0,1:T(8,128)(2,1)S(1)} %convolution_convert_fusion.2), channel_id=1, replica_groups=mesh['seq'=32,'exp'=8] {'seq'}, dimensions={1}, use_global_device_ids=true | all-gather | bytes 101376 | tf_op jit(solution)/shard_map/all_gather | solution.py:134
  339.8 1.0 convolution_convert_fusion
  340.8 8.5 %all-to-all-start = ((bf16[8,2,8,1024]{3,2,1,0:T(8,128)(2,1)}), bf16[8,2,8,1024]{3,2,1,0:T(8,128)(2,1)S(1)}, u32[]{:S(2)}, u32[]{:S(2)}) async-start(bf16[8,2,8,1024]{3,2,1,0:T(8,128)(2,1)} %bitcast.13), calls=%async_computation | async-start | bytes 524288 | tf_op jit(solution)/shard_map/all_to_all | solution.py:156
  349.3 12.3 %all-to-all-done = bf16[8,2,8,1024]{3,2,1,0:T(8,128)(2,1)S(1)} async-done(((bf16[8,2,8,1024]{3,2,1,0:T(8,128)(2,1)}), bf16[8,2,8,1024]{3,2,1,0:T(8,128)(2,1)S(1)}, u32[]{:S(2)}, u32[]{:S(2)}) %all-to-all-start) | async-done | bytes 262176 | tf_op jit(solution)/shard_map/all_to_all | solution.py:156
  361.7 0.4 convolution_bitcast_fusion.2
  362.2 0.8 multiply_convert_fusion
  363.1 106.3 %all-reduce.6.cloned.1.call-done = bf16[8,2,8,1024]{3,2,1,0:T(8,128)(2,1)} async-done(((bf16[8,2,8,1024]{3,2,1,0:T(8,128)(2,1)}), bf16[8,2,8,1024]{3,2,1,0:T(8,128)(2,1)}) %all-reduce.6.cloned.1.call-update) | async-done | bytes 262160 | tf_op jit(solution)/shard_map/psum | solution.py:163
  469.3 7.0 %all-to-all-start.1 = ((bf16[8,2,8,1024]{3,2,1,0:T(8,128)(2,1)}), bf16[8,2,8,1024]{3,2,1,0:T(8,128)(2,1)S(1)}, u32[]{:S(2)}, u32[]{:S(2)}) async-start(bf16[8,2,8,1024]{3,2,1,0:T(8,128)(2,1)} %all-reduce.6.cloned.1.call-done), calls=%async_computation.1 | async-start | bytes 524288 | tf_op jit(solution)/shard_map/all_to_all | solution.py:164
  476.3 12.2 %all-to-all-done.1 = bf16[8,2,8,1024]{3,2,1,0:T(8,128)(2,1)S(1)} async-done(((bf16[8,2,8,1024]{3,2,1,0:T(8,128)(2,1)}), bf16[8,2,8,1024]{3,2,1,0:T(8,128)(2,1)S(1)}, u32[]{:S(2)}, u32[]{:S(2)}) %all-to-all-start.1) | async-done | bytes 262176 | tf_op jit(solution)/shard_map/all_to_all | solution.py:164
  488.5 0.3 fusion.5
  488.8 0.7 reshape.164
  (74 shorter events, 4.5 us)
Async XLA Ops:
  6.5 355.1 %copy-start = (bf16[2,1,176,1024]{3,2,1,0:T(8,128)(2,1)S(1)}, bf16[2,1,176,1024]{3,2,1,0:T(8,128)(2,1)}, u32[]{:S(2)}) copy-start(bf16[2,1,176,1024]{3,2,1,0:T(8,128)(2,1)} %param.24) | copy-start | bytes 2162692
  6.5 291.9 %all-reduce.4.cloned.1.call-start = ((), (), s32[]{:S(2)}) async-start(), calls=%async_computation.2 | async-start | bytes 196608 | tf_op jit(solution)/shard_map/psum | solution.py:125
  16.8 4.9 copy-start.2
  16.8 4.9 copy-start.6
  47.4 3.7 copy-start.3
  168.5 128.5 %copy-start.8 = (s32[12,4,2]{0,2,1:T(2,128)S(1)}, s32[12,4,2]{0,2,1:T(2,128)}, u32[]{:S(2)}) copy-start(s32[12,4,2]{0,2,1:T(2,128)} %param.22) | copy-start | bytes 1156
  168.5 128.7 %copy-start.9 = (s32[1,48]{1,0:T(1,128)S(1)}, s32[1,48]{1,0:T(1,128)}, u32[]{:S(2)}) copy-start(s32[1,48]{1,0:T(1,128)} %param.23) | copy-start | bytes 580
  168.5 130.9 %copy-start.4 = (bf16[32,1024]{1,0:T(8,128)(2,1)S(1)}, bf16[32,1024]{1,0:T(8,128)(2,1)}, u32[]{:S(2)}) copy-start(bf16[32,1024]{1,0:T(8,128)(2,1)} %param.19) | copy-start | bytes 196612
  168.5 170.9 %copy-start.7 = (f32[1024]{0:T(1024)S(1)}, f32[1024]{0:T(1024)}, u32[]{:S(2)}) copy-start(f32[1024]{0:T(1024)} %param.20) | copy-start | bytes 12292
  172.3 167.3 %copy-start.5 = (bf16[1024,16]{0,1:T(8,128)(2,1)S(1)}, bf16[1024,16]{0,1:T(8,128)(2,1)}, u32[]{:S(2)}) copy-start(bf16[1024,16]{0,1:T(8,128)(2,1)} %param.21) | copy-start | bytes 98308
  172.3 189.8 %copy-start.1 = (bf16[1,176,1024]{2,1,0:T(8,128)(2,1)S(1)}, bf16[1,176,1024]{2,1,0:T(8,128)(2,1)}, u32[]{:S(2)}) copy-start(bf16[1,176,1024]{2,1,0:T(8,128)(2,1)} %param.25) | copy-start | bytes 1081348
  340.8 20.9 %all-to-all-start = ((bf16[8,2,8,1024]{3,2,1,0:T(8,128)(2,1)}), bf16[8,2,8,1024]{3,2,1,0:T(8,128)(2,1)S(1)}, u32[]{:S(2)}, u32[]{:S(2)}) async-start(bf16[8,2,8,1024]{3,2,1,0:T(8,128)(2,1)} %bitcast.13), calls=%async_computation | async-start | bytes 524288 | tf_op jit(solution)/shard_map/all_to_all | solution.py:156
  349.3 120.1 %all-reduce.6.cloned.1.call-start = ((), (), s32[]{:S(2)}) async-start(), calls=%async_computation.3 | async-start | bytes 524288 | tf_op jit(solution)/shard_map/psum | solution.py:163
  469.3 19.2 %all-to-all-start.1 = ((bf16[8,2,8,1024]{3,2,1,0:T(8,128)(2,1)}), bf16[8,2,8,1024]{3,2,1,0:T(8,128)(2,1)S(1)}, u32[]{:S(2)}, u32[]{:S(2)}) async-start(bf16[8,2,8,1024]{3,2,1,0:T(8,128)(2,1)} %all-reduce.6.cloned.1.call-done), calls=%async_computation.1 | async-start | bytes 524288 | tf_op jit(solution)/shard_map/all_to_all | solution.py:164
Sparse Core Ops, SparseCore 0:
  173.3 125.0 all-reduce.3
  363.2 106.0 all-reduce.5
where the time goes:
time: 497 us; the launch traced here: 496 us
  blocking collectives  297 us (60%)
  waiting for transfers between devices  131 us (26%)
  local copies, waits for them, and re-layouts  22.1 us (4%)
  starting transfers between devices  15.5 us (3%)
  between operations  13.8 us (3%)
  matrix products  10.1 us (2%)
  other arithmetic  6.1 us (1%)
    psum x1, blocking collectives, body(): lax.psum((weight_sum * factor).astype(jnp.bfloat16), 'seq')  124 us
    pmax x1, blocking collectives, body(): overall = lax.pmax(peak_score, 'seq')  109 us
    psum x1, waiting for transfers between devices, body(): summed = lax.psum(expert_part.astype(jnp.bfloat16), 'seq')  106 us
    all_gather x1, blocking collectives, body(): projected = lax.all_gather(local_proj, 'seq', axis=1, tiled=True)  39.6 us
    all_gather x1, blocking collectives, body(): lax.all_gather(local_mix, 'seq', axis=1, tiled=True)  24.9 us
    all_to_all x1, waiting for transfers between devices, body(): lax.all_to_all(buffer, 'exp', split_axis=0, concat_axis=0, tiled=True)  12.3 us
    all_to_all x1, waiting for transfers between devices, body(): lax.all_to_all(summed, 'exp', split_axis=0, concat_axis=0, tiled=True)  12.2 us
    slice x2, local copies, waits for them, and re-layouts, body(): cache_values = window_cache[1].reshape(requests, slot_span, HEADS, HD)  11.3 us
  transfers between devices with their start and end apart: 4, of which 4 were waited for; matrix products, arithmetic and copies ran while one was open for 0% of the time, Pallas kernels for 0%

commit v1 on v0

--- a/solution.py
+++ b/solution.py
@@ -131,7 +131,9 @@
         contract,
         preferred_element_type=jnp.float32,
     ).astype(jnp.bfloat16)
-    projected = lax.all_gather(local_proj, "seq", axis=1, tiled=True)
+    projected = jnp.concatenate(
+        lax.all_to_all(jnp.stack([local_proj] * lax.axis_size("seq")), "seq", 0, 0), axis=1
+    )
     residual = flat_rows.astype(jnp.float32) + projected.astype(jnp.float32)
     normed_moe = rms_scale(residual, moe_gain)
     logits = jnp.dot(normed_moe, router, preferred_element_type=jnp.float32)

time: 497 us -> 487 us (0.980)
  blocking collectives: 297 us -> 258 us
  starting transfers between devices: 15.5 us -> 36.7 us
  waiting for transfers between devices: 131 us -> 137 us
    all_gather x1 -> x0, blocking collectives: 39.6 us -> none  [body(): projected = lax.all_gather(local_proj, 'seq', axis=1, tiled=True)]
    all_to_all x0 -> x1, starting transfers between devices: none -> 21.2 us  [body(): lax.all_to_all(jnp.stack([local_proj] * lax.axis_size('seq')), 'seq', 0, 0)]
    all_to_all x0 -> x1, waiting for transfers between devices: none -> 6.28 us  [body(): lax.all_to_all(jnp.stack([local_proj] * lax.axis_size('seq')), 'seq', 0, 0)]
  transfers between devices with their start and end apart: 4 -> 5, of which waited for: 4 -> 5; matrix products, arithmetic and copies ran while one was open for 0% -> 0% of each run, Pallas kernels for 0% -> 0%
where the time goes in v1:
time: 487 us; the launch traced here: 486 us
  blocking collectives  258 us (53%)
  waiting for transfers between devices  137 us (28%)
  starting transfers between devices  36.7 us (8%)
  local copies, waits for them, and re-layouts  24 us (5%)
  between operations  13.9 us (3%)
  matrix products  10.1 us (2%)
  other arithmetic  6.9 us (1%)
    psum x1, blocking collectives, body(): lax.psum((weight_sum * factor).astype(jnp.bfloat16), 'seq')  124 us
    pmax x1, blocking collectives, body(): overall = lax.pmax(peak_score, 'seq')  109 us
    psum x1, waiting for transfers between devices, body(): summed = lax.psum(expert_part.astype(jnp.bfloat16), 'seq')  105 us
    all_gather x1, blocking collectives, body(): lax.all_gather(local_mix, 'seq', axis=1, tiled=True)  24.9 us
    all_to_all x1, starting transfers between devices, body(): lax.all_to_all(jnp.stack([local_proj] * lax.axis_size('seq')), 'seq', 0, 0)  21.2 us
    all_to_all x1, waiting for transfers between devices, body(): lax.all_to_all(summed, 'exp', split_axis=0, concat_axis=0, tiled=True)  12.2 us
    all_to_all x1, waiting for transfers between devices, body(): lax.all_to_all(buffer, 'exp', split_axis=0, concat_axis=0, tiled=True)  12.1 us
    slice x2, local copies, waits for them, and re-layouts, body(): cache_values = window_cache[1].reshape(requests, slot_span, HEADS, HD)  11.3 us
  transfers between devices with their start and end apart: 5, of which 5 were waited for; matrix products, arithmetic and copies ran while one was open for 0% of the time, Pallas kernels for 0%

profile of v1, /device:TPU:2, one launch (start us, length us, event | category | flops | bytes accessed | tf_op | source)
XLA Modules:
  0.0 486.0 jit_solution(486405315053313673)
XLA Ops:
  6.5 0.8 add_select_fusion
  7.3 0.7 add_minimum_fusion
  8.0 0.9 reshape.182
  8.9 1.0 multiply_reduce_fusion.1
  10.2 6.6 %fusion.66 = (bf16[1,12,128,1024]{3,2,1,0:T(8,128)(2,1)}, bf16[1,12,128,1024]{3,2,1,0:T(8,128)(2,1)}) fusion(bf16[2,12,128,1024]{3,2,1,0:T(8,128)(2,1)} %param.16), kind=kLoop, calls=%fused_computation.112 | loop fusion | bytes 12582912 | tf_op jit(solution)/shard_map/slice | solution.py:75
  16.8 4.8 copy.83
  21.9 24.9 %all-gather = bf16[32,96,48]{1,2,0:T(8,128)(2,1)S(1)} all-gather(bf16[1,96,48]{1,2,0:T(8,128)(2,1)S(1)} %fusion.6), channel_id=1, replica_groups=mesh['seq'=32,'exp'=8] {'seq'}, dimensions={0}, use_global_device_ids=true | all-gather | bytes 304128 | tf_op jit(solution)/shard_map/all_gather | solution.py:65
  46.9 0.5 reshape.186
  48.0 2.9 select_reduce_fusion.1
  51.6 0.5 select_reduce_fusion
  52.4 109.0 %pmax.7 = f32[12,4,16]{2,1,0:T(4,128)S(1)} all-reduce(f32[12,4,16]{2,1,0:T(4,128)S(1)} %max.9), channel_id=1, replica_groups=mesh['seq'=32,'exp'=8] {'seq'}, use_global_device_ids=true, to_apply=%region_4.5 | all-reduce | flops 768 | bytes 6144 | tf_op jit(solution)/shard_map/pmax | solution.py:121
  161.4 0.5 fusion.16
  162.0 0.5 fusion.18
  163.1 4.7 copy.89
  168.0 0.5 convolution_bitcast_fusion
  168.5 3.7 fusion.4
  172.3 0.8 convert_element_type.123
  173.1 123.8 %psum.22 = bf16[12,4,16]{2,1,0:T(4,128)(2,1)S(1)} all-reduce(bf16[12,4,16]{2,1,0:T(4,128)(2,1)S(1)} %get-tuple-element.7), channel_id=1, replica_groups=mesh['seq'=32,'exp'=8] {'seq'}, use_global_device_ids=true, to_apply=%region_8.9 | all-reduce | flops 768 | bytes 3072 | tf_op jit(solution)/shard_map/psum | solution.py:124
  297.6 0.8 all-reduce.4.cloned.1.call-done
  298.4 0.9 multiply_convert_fusion.2
  299.6 1.0 reshape.191
  300.6 21.2 %all-to-all-start = ((bf16[32,2,768]{2,1,0:T(2,128)(2,1)}), bf16[32,2,768]{2,1,0:T(2,128)(2,1)S(1)}, u32[]{:S(2)}, u32[]{:S(2)}) async-start(bf16[32,2,768]{2,1,0:T(2,128)(2,1)} %reshape.191), calls=%async_computation | async-start | bytes 196608 | tf_op jit(solution)/shard_map/all_to_all | solution.py:135
  322.0 6.3 %all-to-all-done = bf16[32,2,768]{2,1,0:T(2,128)(2,1)S(1)} async-done(((bf16[32,2,768]{2,1,0:T(2,128)(2,1)}), bf16[32,2,768]{2,1,0:T(2,128)(2,1)S(1)}, u32[]{:S(2)}, u32[]{:S(2)}) %all-to-all-start) | async-done | bytes 98336 | tf_op jit(solution)/shard_map/all_to_all | solution.py:135
  328.8 0.7 copy.97
  330.6 1.0 convolution_convert_fusion
  331.6 8.5 %all-to-all-start.1 = ((bf16[8,2,8,1024]{3,2,1,0:T(8,128)(2,1)}), bf16[8,2,8,1024]{3,2,1,0:T(8,128)(2,1)S(1)}, u32[]{:S(2)}, u32[]{:S(2)}) async-start(bf16[8,2,8,1024]{3,2,1,0:T(8,128)(2,1)} %bitcast.15), calls=%async_computation.1 | async-start | bytes 524288 | tf_op jit(solution)/shard_map/all_to_all | solution.py:158
  340.1 12.1 %all-to-all-done.1 = bf16[8,2,8,1024]{3,2,1,0:T(8,128)(2,1)S(1)} async-done(((bf16[8,2,8,1024]{3,2,1,0:T(8,128)(2,1)}), bf16[8,2,8,1024]{3,2,1,0:T(8,128)(2,1)S(1)}, u32[]{:S(2)}, u32[]{:S(2)}) %all-to-all-start.1) | async-done | bytes 262176 | tf_op jit(solution)/shard_map/all_to_all | solution.py:158
  352.8 0.8 multiply_convert_fusion
  353.6 105.3 %all-reduce.6.cloned.1.call-done = bf16[8,2,8,1024]{3,2,1,0:T(8,128)(2,1)} async-done(((bf16[8,2,8,1024]{3,2,1,0:T(8,128)(2,1)}), bf16[8,2,8,1024]{3,2,1,0:T(8,128)(2,1)}) %all-reduce.6.cloned.1.call-update) | async-done | bytes 262160 | tf_op jit(solution)/shard_map/psum | solution.py:165
  458.9 7.0 %all-to-all-start.2 = ((bf16[8,2,8,1024]{3,2,1,0:T(8,128)(2,1)}), bf16[8,2,8,1024]{3,2,1,0:T(8,128)(2,1)S(1)}, u32[]{:S(2)}, u32[]{:S(2)}) async-start(bf16[8,2,8,1024]{3,2,1,0:T(8,128)(2,1)} %all-reduce.6.cloned.1.call-done), calls=%async_computation.2 | async-start | bytes 524288 | tf_op jit(solution)/shard_map/all_to_all | solution.py:166
  465.9 12.2 %all-to-all-done.2 = bf16[8,2,8,1024]{3,2,1,0:T(8,128)(2,1)S(1)} async-done(((bf16[8,2,8,1024]{3,2,1,0:T(8,128)(2,1)}), bf16[8,2,8,1024]{3,2,1,0:T(8,128)(2,1)S(1)}, u32[]{:S(2)}, u32[]{:S(2)}) %all-to-all-start.2) | async-done | bytes 262176 | tf_op jit(solution)/shard_map/all_to_all | solution.py:166
  478.4 0.7 add_convert_fusion
  (85 shorter events, 6.4 us)
Async XLA Ops:
  6.5 345.7 %copy-start = (bf16[2,1,176,1024]{3,2,1,0:T(8,128)(2,1)S(1)}, bf16[2,1,176,1024]{3,2,1,0:T(8,128)(2,1)}, u32[]{:S(2)}) copy-start(bf16[2,1,176,1024]{3,2,1,0:T(8,128)(2,1)} %param.24) | copy-start | bytes 2162692
  6.5 291.9 %all-reduce.4.cloned.1.call-start = ((), (), s32[]{:S(2)}) async-start(), calls=%async_computation.3 | async-start | bytes 196608 | tf_op jit(solution)/shard_map/psum | solution.py:125
  16.8 4.9 %copy-start.3 = (bf16[96,1024]{1,0:T(8,128)(2,1)S(1)}, bf16[96,1024]{1,0:T(8,128)(2,1)}, u32[]{:S(2)}) copy-start(bf16[96,1024]{1,0:T(8,128)(2,1)} %param.15) | copy-start | bytes 589828
  16.8 4.9 %copy-start.7 = (f32[1024]{0:T(1024)S(1)}, f32[1024]{0:T(1024)}, u32[]{:S(2)}) copy-start(f32[1024]{0:T(1024)} %param.14) | copy-start | bytes 12292
  47.4 3.7 copy-start.4
  168.5 128.5 %copy-start.9 = (s32[12,4,2]{0,2,1:T(2,128)S(1)}, s32[12,4,2]{0,2,1:T(2,128)}, u32[]{:S(2)}) copy-start(s32[12,4,2]{0,2,1:T(2,128)} %param.22) | copy-start | bytes 1156
  168.5 130.9 %copy-start.5 = (bf16[32,1024]{1,0:T(8,128)(2,1)S(1)}, bf16[32,1024]{1,0:T(8,128)(2,1)}, u32[]{:S(2)}) copy-start(bf16[32,1024]{1,0:T(8,128)(2,1)} %param.19) | copy-start | bytes 196612
  168.5 153.3 %copy-start.10 = (s32[1,48]{1,0:T(1,128)S(1)}, s32[1,48]{1,0:T(1,128)}, u32[]{:S(2)}) copy-start(s32[1,48]{1,0:T(1,128)} %param.23) | copy-start | bytes 580
  299.3 30.6 %copy-start.1 = (bf16[12,4,1024]{2,1,0:T(4,128)(2,1)S(1)}, bf16[12,4,1024]{2,1,0:T(4,128)(2,1)}, u32[]{:S(2)}) copy-start(bf16[12,4,1024]{2,1,0:T(4,128)(2,1)} %param.13) | copy-start | bytes 294916
  299.4 30.8 %copy-start.8 = (f32[1024]{0:T(1024)S(1)}, f32[1024]{0:T(1024)}, u32[]{:S(2)}) copy-start(f32[1024]{0:T(1024)} %param.20) | copy-start | bytes 12292
  299.6 30.7 %copy-start.6 = (bf16[1024,16]{0,1:T(8,128)(2,1)S(1)}, bf16[1024,16]{0,1:T(8,128)(2,1)}, u32[]{:S(2)}) copy-start(bf16[1024,16]{0,1:T(8,128)(2,1)} %param.21) | copy-start | bytes 98308
  300.6 27.6 %all-to-all-start = ((bf16[32,2,768]{2,1,0:T(2,128)(2,1)}), bf16[32,2,768]{2,1,0:T(2,128)(2,1)S(1)}, u32[]{:S(2)}, u32[]{:S(2)}) async-start(bf16[32,2,768]{2,1,0:T(2,128)(2,1)} %reshape.191), calls=%async_computation | async-start | bytes 196608 | tf_op jit(solution)/shard_map/all_to_all | solution.py:135
  328.6 23.9 %copy-start.2 = (bf16[1,176,1024]{2,1,0:T(8,128)(2,1)S(1)}, bf16[1,176,1024]{2,1,0:T(8,128)(2,1)}, u32[]{:S(2)}) copy-start(bf16[1,176,1024]{2,1,0:T(8,128)(2,1)} %param.25) | copy-start | bytes 1081348
  331.6 20.6 %all-to-all-start.1 = ((bf16[8,2,8,1024]{3,2,1,0:T(8,128)(2,1)}), bf16[8,2,8,1024]{3,2,1,0:T(8,128)(2,1)S(1)}, u32[]{:S(2)}, u32[]{:S(2)}) async-start(bf16[8,2,8,1024]{3,2,1,0:T(8,128)(2,1)} %bitcast.15), calls=%async_computation.1 | async-start | bytes 524288 | tf_op jit(solution)/shard_map/all_to_all | solution.py:158
  340.0 118.9 %all-reduce.6.cloned.1.call-start = ((), (), s32[]{:S(2)}) async-start(), calls=%async_computation.4 | async-start | bytes 524288 | tf_op jit(solution)/shard_map/psum | solution.py:165
  458.9 19.2 %all-to-all-start.2 = ((bf16[8,2,8,1024]{3,2,1,0:T(8,128)(2,1)}), bf16[8,2,8,1024]{3,2,1,0:T(8,128)(2,1)S(1)}, u32[]{:S(2)}, u32[]{:S(2)}) async-start(bf16[8,2,8,1024]{3,2,1,0:T(8,128)(2,1)} %all-reduce.6.cloned.1.call-done), calls=%async_computation.2 | async-start | bytes 524288 | tf_op jit(solution)/shard_map/all_to_all | solution.py:166
Sparse Core Ops, SparseCore 0:
  173.3 125.0 all-reduce.3
  353.7 105.1 all-reduce.5
